TPU v7x, 32 devices: a whole 2x2x4 slice. The times are simulated.
32 devices in a mesh: dp: 16 (over z, y, x), tensor: 2 (over core).
Axes of the slice: x: 2, y: 2, z: 4, core: 2. Of those that a mesh axis runs over, the one named last changes fastest.
Arguments:
- tokens: bfloat16 [16384, 768], P('dp'), may hold values from -6 to 6
- cotangent: bfloat16 [16384, 768], P('dp'), may hold values from -6 to 6
- lengths: int32 [32], P('dp'), may hold values from 113 to 512, as said below
- proj_weight: float32 [2, 768, 3, 768], P(None, 'dp', None, 'tensor'), may hold values from -0.21875 to 0.21875
- out_weight: float32 [2, 768, 768], P(None, 'dp', 'tensor'), may hold values from -0.875 to 0.875
- up_weight: float32 [2, 768, 3072], P(None, 'dp', 'tensor'), may hold values from -0.21875 to 0.21875
- down_weight: float32 [2, 768, 3072], P(None, 'dp', 'tensor'), may hold values from -0.109375 to 0.109375
- small_params: float32 [2, 8448], replicated, may hold values from -0.8 to 1.4
- proj_first: float32 [2, 768, 3, 768], P(None, 'dp', None, 'tensor'), may hold values from -0.00018310547 to 0.00018310547
- proj_second: float32 [2, 768, 3, 768], P(None, 'dp', None, 'tensor'), may hold values from 3.527916e-11 to 3.52791626e-09
- out_first: float32 [2, 768, 768], P(None, 'dp', 'tensor'), may hold values from -0.00018310547 to 0.00018310547
- out_second: float32 [2, 768, 768], P(None, 'dp', 'tensor'), may hold values from 7.0558325e-12 to 7.0558325e-10
- up_first: float32 [2, 768, 3072], P(None, 'dp', 'tensor'), may hold values from -0.00018310547 to 0.00018310547
- up_second: float32 [2, 768, 3072], P(None, 'dp', 'tensor'), may hold values from 3.527916e-11 to 3.52791626e-09
- down_first: float32 [2, 768, 3072], P(None, 'dp', 'tensor'), may hold values from -0.00018310547 to 0.00018310547
- down_second: float32 [2, 768, 3072], P(None, 'dp', 'tensor'), may hold values from 3.527916e-11 to 3.52791626e-09
- small_first: float32 [2, 8448], replicated, may hold values from -0.00018310547 to 0.00018310547
- small_second: float32 [2, 8448], replicated, may hold values from 3.527916e-11 to 5.644666e-10
Outputs:
- activations: float32 [16384, 768], P('dp')
- input_grad: float32 [16384, 768], P('dp')
- grad_norm: float32 [], replicated
- proj_first_new: float32 [2, 768, 3, 768], P(None, 'dp', None, 'tensor')
- proj_second_new: float32 [2, 768, 3, 768], P(None, 'dp', None, 'tensor')
- proj_weight_new: float32 [2, 768, 3, 768], P(None, 'dp', None, 'tensor')
- out_first_new: float32 [2, 768, 768], P(None, 'dp', 'tensor')
- out_second_new: float32 [2, 768, 768], P(None, 'dp', 'tensor')
- out_weight_new: float32 [2, 768, 768], P(None, 'dp', 'tensor')
- up_first_new: float32 [2, 768, 3072], P(None, 'dp', 'tensor')
- up_second_new: float32 [2, 768, 3072], P(None, 'dp', 'tensor')
- up_weight_new: float32 [2, 768, 3072], P(None, 'dp', 'tensor')
- down_first_new: float32 [2, 768, 3072], P(None, 'dp', 'tensor')
- down_second_new: float32 [2, 768, 3072], P(None, 'dp', 'tensor')
- down_weight_new: float32 [2, 768, 3072], P(None, 'dp', 'tensor')
- small_first_new: float32 [2, 8448], replicated
- small_second_new: float32 [2, 8448], replicated
- small_params_new: float32 [2, 8448], replicated
Inputs may be any that keep to these rules, and one draw needn't show every extreme that they name: `lengths`: each length is 512, 256 or 128, reduced by less than max(1, 16); the first sequence has length 512.
All inputs are finite; a program needn't handle non-finite values.
Results may differ from a plain program's by a relative error of at most 0.03.
The roundings to bfloat16 on the way count: a program that leaves them out, or rounds other values in their place, can miss the bound.
Values may be sent and summed in bfloat16 or wider, within the bound.
No kernel may reach another device: no remote copies, remote signals or barrier semaphores. Data moves between devices by JAX's collectives and lax.ppermute only.
A program may use at most 192 MiB of HBM per device.

v0:
```python
from functools import partial
import math
import jax
import jax.numpy as jnp
from jax import lax
from jax.sharding import PartitionSpec as P

D = 768
HEADS = 12
FF = 3072
beta_one = 0.9
beta_two = 0.999
adam_eps = 1e-06
decay_rate = 0.01
matrix_rate = 1.0
vector_rate = 0.3
clip_norm = 1.0
step_count = 10.0
norm_eps = 1e-06
masked_score = -1e30


def layer_norm(values, norm_gain, norm_shift):
    average = jnp.mean(values, axis=-1, keepdims=True)
    centered = values - average
    variance = jnp.mean(centered * centered, axis=-1, keepdims=True)
    return centered * lax.rsqrt(variance + norm_eps) * norm_gain + norm_shift


def split_vector(packed):
    bounds = [0, D, 2 * D, 2 * D + FF, 3 * D + FF, 4 * D + FF, 5 * D + FF, 6 * D + FF, 7 * D + FF]
    return [packed[bounds[place] : bounds[place + 1]] for place in range(8)]


def head_scores(query, keys, score_scale):
    return jnp.einsum("qhe,khe->hqk", query, keys, preferred_element_type=jnp.float32) * score_scale


def total_scores(pairs, score_scale):
    score_total = head_scores(pairs[0], pairs[1], score_scale)
    for place in range(2, len(pairs), 2):
        score_total = score_total + head_scores(pairs[place], pairs[place + 1], score_scale)
    return score_total


def attend_forward(block_item, score_scale):
    key_valid, value_rows = (block_item[0], block_item[1])
    score_total = total_scores(block_item[2:], score_scale)
    masked = jnp.where(key_valid[None, None, :], score_total, masked_score)
    row_max = jnp.max(masked, axis=-1, keepdims=True)
    exp_terms = jnp.exp(masked - row_max)
    row_sum = jnp.sum(exp_terms, axis=-1, keepdims=True)
    soft_low = (exp_terms / row_sum).astype(jnp.bfloat16)
    context = jnp.einsum("hqk,khe->qhe", soft_low, value_rows, preferred_element_type=jnp.float32)
    return (context.astype(jnp.bfloat16), (row_max + jnp.log(row_sum))[..., 0])


def attend_backward(block_item, score_scale, with_later, keep_total):
    key_valid, value_rows, log_norm, context_grad = (
        block_item[0],
        block_item[1],
        block_item[2],
        block_item[3],
    )
    rest = block_item[4:]
    if with_later:
        later = rest[0]
        pairs = rest[1:]
    else:
        pairs = rest
    score_total = total_scores(pairs, score_scale)
    soft = jnp.where(key_valid[None, None, :], jnp.exp(score_total - log_norm[..., None]), 0.0)
    soft_grad = jnp.einsum(
        "qhe,khe->hqk", context_grad, value_rows, preferred_element_type=jnp.float32
    )
    total_grad = soft * (soft_grad - jnp.sum(soft * soft_grad, axis=-1, keepdims=True))
    if with_later:
        total_grad = total_grad + later
    total_low = total_grad.astype(jnp.bfloat16)
    query_grad = (
        jnp.einsum("hqk,khe->qhe", total_low, pairs[1], preferred_element_type=jnp.float32)
        * score_scale
    )
    key_grad = (
        jnp.einsum("hqk,qhe->khe", total_low, pairs[0], preferred_element_type=jnp.float32)
        * score_scale
    )
    value_grad = jnp.einsum(
        "hqk,qhe->khe", soft.astype(jnp.bfloat16), context_grad, preferred_element_type=jnp.float32
    )
    results = (query_grad, key_grad, value_grad)
    if keep_total:
        results = results + (total_grad,)
    return results


def adam_parts(gradient, first, second, factor):
    clipped = gradient * factor
    first_new = beta_one * first + (1.0 - beta_one) * clipped
    second_new = beta_two * second + (1.0 - beta_two) * clipped * clipped
    first_hat = first_new / (1.0 - beta_one**step_count)
    second_hat = second_new / (1.0 - beta_two**step_count)
    return (first_new, second_new, first_hat / (jnp.sqrt(second_hat) + adam_eps))


def local(
    tokens,
    cotangent,
    lengths,
    proj_weight,
    out_weight,
    up_weight,
    down_weight,
    small_params,
    proj_first,
    proj_second,
    out_first,
    out_second,
    up_first,
    up_second,
    down_first,
    down_second,
    small_first,
    small_second,
):
    layers = proj_weight.shape[0]
    seq_count = lengths.shape[0]
    seq_len = tokens.shape[0] // seq_count
    local_width = proj_weight.shape[3]
    head_dim = D // HEADS
    local_heads = local_width // head_dim
    hidden_local = up_weight.shape[2]
    score_scale = 1.0 / math.sqrt(head_dim)
    share_scale = 1.0 / lax.axis_size("tensor")
    tensor_rank = lax.axis_index("tensor")
    proj_full, out_full, up_full, down_full = (
        lax.all_gather(proj_weight.astype(jnp.bfloat16), "dp", axis=1, tiled=True),
        lax.all_gather(out_weight.astype(jnp.bfloat16), "dp", axis=1, tiled=True),
        lax.all_gather(up_weight.astype(jnp.bfloat16), "dp", axis=1, tiled=True),
        lax.all_gather(down_weight.astype(jnp.bfloat16), "dp", axis=1, tiled=True),
    )
    positions = jnp.arange(seq_len)
    key_valid = positions[None, :] < lengths[:, None]
    row_valid = key_valid.reshape(-1, 1)

    def own_part(vector, width):
        return lax.dynamic_slice_in_dim(vector, tensor_rank * width, width)

    def place_part(local_values, full_width):
        return lax.dynamic_update_slice_in_dim(
            jnp.zeros((full_width,), jnp.float32),
            local_values,
            tensor_rank * local_values.shape[0],
            0,
        )

    def heads_view(rows):
        return rows.reshape(seq_count, seq_len, local_heads, head_dim)

    hidden = tokens.astype(jnp.float32)
    saved = []
    for layer_at in range(layers):
        bias_v, bias_o, bias_up, bias_down, gain_one, shift_one, gain_two, shift_two = split_vector(
            small_params[layer_at]
        )
        input_low = hidden.astype(jnp.bfloat16)
        projected = jnp.einsum(
            "td,dcf->tcf", input_low, proj_full[layer_at], preferred_element_type=jnp.float32
        )
        query_low = projected[:, 0].astype(jnp.bfloat16)
        key_low = projected[:, 1].astype(jnp.bfloat16)
        value_low = (projected[:, 2] + own_part(bias_v, local_width)).astype(jnp.bfloat16)
        pairs = [heads_view(query_low), heads_view(key_low)]
        for earlier in reversed(saved):
            pairs += [heads_view(earlier["query"]), heads_view(earlier["keys"])]
        context_low, log_norm = lax.map(
            partial(attend_forward, score_scale=score_scale),
            (key_valid, heads_view(value_low)) + tuple(pairs),
        )
        context_low = context_low.reshape(-1, local_width)
        attended = lax.psum(
            jnp.einsum(
                "tf,df->td", context_low, out_full[layer_at], preferred_element_type=jnp.float32
            ).astype(jnp.bfloat16),
            "tensor",
        ).astype(jnp.float32)
        first_in = hidden + attended + bias_o
        first_out = layer_norm(first_in, gain_one, shift_one)
        first_low = first_out.astype(jnp.bfloat16)
        before_act = jnp.einsum(
            "td,df->tf", first_low, up_full[layer_at], preferred_element_type=jnp.float32
        ) + own_part(bias_up, hidden_local)
        act_low = jax.nn.gelu(before_act, approximate=False).astype(jnp.bfloat16)
        returned = lax.psum(
            jnp.einsum(
                "tf,df->td", act_low, down_full[layer_at], preferred_element_type=jnp.float32
            ).astype(jnp.bfloat16),
            "tensor",
        ).astype(jnp.float32)
        second_in = first_out + returned + bias_down
        saved.append(
            {
                "layer_input": input_low,
                "query": query_low,
                "keys": key_low,
                "value_rows": value_low,
                "log_norm": log_norm,
                "context": context_low,
                "first_in": first_in,
                "first_low": first_low,
                "before_act": before_act,
                "act_low": act_low,
                "second_in": second_in,
            }
        )
        hidden = layer_norm(second_in, gain_two, shift_two)
    grad_rows = jnp.where(row_valid, cotangent.astype(jnp.float32), 0.0)
    proj_grads = [None] * layers
    out_grads = [None] * layers
    up_grads = [None] * layers
    down_grads = [None] * layers
    small_grads = [None] * layers
    later_total = None
    for layer_at in reversed(range(layers)):
        kept = saved[layer_at]
        bias_v, bias_o, bias_up, bias_down, gain_one, shift_one, gain_two, shift_two = split_vector(
            small_params[layer_at]
        )
        second_in_grad, gain_two_grad, shift_two_grad = jax.vjp(
            layer_norm, kept["second_in"], gain_two, shift_two
        )[1](grad_rows)
        down_in_low = second_in_grad.astype(jnp.bfloat16)
        down_grads[layer_at] = jnp.einsum(
            "td,tf->df", down_in_low, kept["act_low"], preferred_element_type=jnp.float32
        )
        act_grad = jnp.einsum(
            "td,df->tf", down_in_low, down_full[layer_at], preferred_element_type=jnp.float32
        )
        before_grad = jax.vjp(partial(jax.nn.gelu, approximate=False), kept["before_act"])[1](
            act_grad
        )[0]
        before_low = before_grad.astype(jnp.bfloat16)
        up_grads[layer_at] = jnp.einsum(
            "td,tf->df", kept["first_low"], before_low, preferred_element_type=jnp.float32
        )
        first_back = lax.psum(
            jnp.einsum(
                "tf,df->td", before_low, up_full[layer_at], preferred_element_type=jnp.float32
            ).astype(jnp.bfloat16),
            "tensor",
        ).astype(jnp.float32)
        first_out_grad = second_in_grad + first_back
        first_in_grad, gain_one_grad, shift_one_grad = jax.vjp(
            layer_norm, kept["first_in"], gain_one, shift_one
        )[1](first_out_grad)
        out_in_low = first_in_grad.astype(jnp.bfloat16)
        out_grads[layer_at] = jnp.einsum(
            "td,tf->df", out_in_low, kept["context"], preferred_element_type=jnp.float32
        )
        context_grad = jnp.einsum(
            "td,df->tf", out_in_low, out_full[layer_at], preferred_element_type=jnp.float32
        ).astype(jnp.bfloat16)
        pairs = [heads_view(kept["query"]), heads_view(kept["keys"])]
        for earlier in reversed(saved[:layer_at]):
            pairs += [heads_view(earlier["query"]), heads_view(earlier["keys"])]
        items = (
            key_valid,
            heads_view(kept["value_rows"]),
            kept["log_norm"],
            heads_view(context_grad),
        )
        with_later = later_total is not None
        if with_later:
            items = items + (later_total,)
        items = items + tuple(pairs)
        results = lax.map(
            partial(
                attend_backward,
                score_scale=score_scale,
                with_later=with_later,
                keep_total=layer_at > 0,
            ),
            items,
        )
        later_total = results[3] if layer_at > 0 else None
        query_grad = results[0].reshape(-1, local_width)
        key_grad = results[1].reshape(-1, local_width)
        value_grad = results[2].reshape(-1, local_width)
        proj_grad_low = jnp.stack([query_grad, key_grad, value_grad], axis=1).astype(jnp.bfloat16)
        proj_grads[layer_at] = jnp.einsum(
            "td,tcf->dcf", kept["layer_input"], proj_grad_low, preferred_element_type=jnp.float32
        )
        input_back = lax.psum(
            jnp.einsum(
                "tcf,dcf->td",
                proj_grad_low,
                proj_full[layer_at],
                preferred_element_type=jnp.float32,
            ).astype(jnp.bfloat16),
            "tensor",
        ).astype(jnp.float32)
        grad_rows = first_in_grad + input_back
        small_grads[layer_at] = jnp.concatenate(
            [
                place_part(jnp.sum(value_grad, axis=0), D),
                share_scale * jnp.sum(first_in_grad, axis=0),
                place_part(jnp.sum(before_grad, axis=0), FF),
                share_scale * jnp.sum(second_in_grad, axis=0),
                share_scale * gain_one_grad,
                share_scale * shift_one_grad,
                share_scale * gain_two_grad,
                share_scale * shift_two_grad,
            ]
        )
    big_totals = (
        jnp.stack(proj_grads),
        jnp.stack(out_grads),
        jnp.stack(up_grads),
        jnp.stack(down_grads),
    )
    small_partial = jnp.stack(small_grads)
    row_count = proj_weight.shape[1]
    summed = lax.psum((big_totals[0], big_totals[1], big_totals[2], big_totals[3]), "dp")
    row_start = lax.axis_index("dp") * row_count
    shares = tuple(
        (lax.dynamic_slice_in_dim(summed_part, row_start, row_count, 1) for summed_part in summed)
    )
    masters = (proj_weight, out_weight, up_weight, down_weight)
    firsts = (proj_first, out_first, up_first, down_first)
    seconds = (proj_second, out_second, up_second, down_second)
    square_part = jnp.sum(shares[0] * shares[0])
    for kind_at in range(1, 4):
        square_part = square_part + jnp.sum(shares[kind_at] * shares[kind_at])
    weight_square = jnp.stack(
        [jnp.sum(master * master, axis=tuple(range(1, master.ndim))) for master in masters]
    )
    square_big, weight_square, small_grad = lax.psum(
        (square_part, weight_square, small_partial), ("dp", "tensor")
    )
    grad_norm = jnp.sqrt(square_big + jnp.sum(small_grad * small_grad))
    factor = clip_norm / jnp.maximum(grad_norm, clip_norm)
    moments = []
    updates = []
    for kind_at in range(4):
        first_new, second_new, direction = adam_parts(
            shares[kind_at], firsts[kind_at], seconds[kind_at], factor
        )
        moments.append((first_new, second_new))
        updates.append(direction + decay_rate * masters[kind_at])
    update_square = jnp.stack(
        [jnp.sum(update * update, axis=tuple(range(1, update.ndim))) for update in updates]
    )
    update_square = lax.psum(update_square, ("dp", "tensor"))
    ratio = jnp.sqrt(weight_square) / jnp.sqrt(update_square)
    outputs = [hidden, grad_rows, grad_norm]
    for kind_at in range(4):
        master = masters[kind_at]
        scaled = ratio[kind_at].reshape((-1,) + (1,) * (master.ndim - 1))
        outputs += [
            moments[kind_at][0],
            moments[kind_at][1],
            master - matrix_rate * scaled * updates[kind_at],
        ]
    small_first_new, small_second_new, small_direction = adam_parts(
        small_grad, small_first, small_second, factor
    )
    outputs += [small_first_new, small_second_new, small_params - vector_rate * small_direction]
    return tuple(outputs)


def solution(mesh):
    placed = (
        P("dp", None),
        P("dp", None),
        P("dp"),
        P(None, "dp", None, "tensor"),
        P(None, "dp", "tensor"),
        P(None, "dp", "tensor"),
        P(None, "dp", "tensor"),
        P(),
        P(None, "dp", None, "tensor"),
        P(None, "dp", None, "tensor"),
        P(None, "dp", "tensor"),
        P(None, "dp", "tensor"),
        P(None, "dp", "tensor"),
        P(None, "dp", "tensor"),
        P(None, "dp", "tensor"),
        P(None, "dp", "tensor"),
        P(),
        P(),
    )
    return jax.shard_map(
        local,
        mesh=mesh,
        in_specs=placed,
        out_specs=(
            P("dp", None),
            P("dp", None),
            P(),
            P(None, "dp", None, "tensor"),
            P(None, "dp", None, "tensor"),
            P(None, "dp", None, "tensor"),
            P(None, "dp", "tensor"),
            P(None, "dp", "tensor"),
            P(None, "dp", "tensor"),
            P(None, "dp", "tensor"),
            P(None, "dp", "tensor"),
            P(None, "dp", "tensor"),
            P(None, "dp", "tensor"),
            P(None, "dp", "tensor"),
            P(None, "dp", "tensor"),
            P(),
            P(),
            P(),
        ),
        check_vma=False,
    )
```

profile of v0, /device:TPU:0, one launch (start us, length us, event | category | flops | bytes accessed | tf_op | source)
XLA Modules:
  0.0 1741.2 jit_solution(10675762374318251473)
XLA Ops:
  13.1 72.2 %all-gather.5.cloned.1.call-done = bf16[2,768,3,384]{3,1,2,0:T(8,128)(2,1)} async-done(((bf16[2,48,3,384]{3,1,2,0:T(8,128)(2,1)}), bf16[2,768,3,384]{3,1,2,0:T(8,128)(2,1)}) %all-gather.5.cloned.1.call-update) | async-done | bytes 3538960 | tf_op jit(solution)/shard_map/all_gather | solution.py:137
  85.3 5.6 fusion.209
  103.5 11.4 while.54
  116.8 26.5 %all-gather.7.cloned.1.call-done = bf16[2,768,384]{2,1,0:T(8,128)(2,1)} async-done(((bf16[2,48,384]{2,1,0:T(8,128)(2,1)}), bf16[2,768,384]{2,1,0:T(8,128)(2,1)}) %all-gather.7.cloned.1.call-update) | async-done | bytes 1179664 | tf_op jit(solution)/shard_map/all_gather | solution.py:138
  150.6 15.8 all-reduce.13.cloned.1.call-done
  169.4 82.1 %all-gather.9.cloned.1.call-done = bf16[2,768,1536]{2,1,0:T(8,128)(2,1)} async-done(((bf16[2,48,1536]{2,1,0:T(8,128)(2,1)}), bf16[2,768,1536]{2,1,0:T(8,128)(2,1)}) %all-gather.9.cloned.1.call-update) | async-done | bytes 4718608 | tf_op jit(solution)/shard_map/all_gather | solution.py:139
  251.5 20.8 %multiply_convert_fusion.1 = (bf16[1024,1536]{1,0:T(8,128)(2,1)}, f32[1024,1536]{1,0:T(8,128)}, f32[1024,1536]{1,0:T(8,128)}) fusion(f32[1536]{0:T(1024)S(1)} %dynamic-slice_reduce_fusion.5, bf16[2,768,1536]{2,1,0:T(8,128)(2,1)} %all-gather.9.cloned.1.call-done, f32[768]{0:T(1024)S(1)} %get-tuple-element.431, f32[768]{0:T(1024)S(1)} %get-tuple-element.432, ...), kind=kOutput, calls=%fused_computation.155 | convolution fusion | flops 2526806016 | bytes 21257216 | tf_op jit(solution)/shard_map/td,df->tf/dot_general | solution.py:190
  272.3 61.6 %all-gather.11.cloned.1.call-done = bf16[2,768,1536]{2,1,0:T(8,128)(2,1)} async-done(((bf16[2,48,1536]{2,1,0:T(8,128)(2,1)}), bf16[2,768,1536]{2,1,0:T(8,128)(2,1)}) %all-gather.11.cloned.1.call-update) | async-done | bytes 4718608 | tf_op jit(solution)/shard_map/all_gather | solution.py:140
  333.9 6.4 fusion.151
  340.5 19.1 %all-reduce.15.cloned.1.call-done = bf16[1024,768]{1,0:T(8,128)(2,1)} async-done(((bf16[1024,768]{1,0:T(8,128)(2,1)}), bf16[1024,768]{1,0:T(8,128)(2,1)}) %all-reduce.15.cloned.1.call-update) | async-done | bytes 1572880 | tf_op jit(solution)/shard_map/psum | solution.py:194
  363.7 3.8 fusion.210
  380.8 14.3 while.55
  400.4 21.7 %all-reduce.17.cloned.1.call-done = bf16[1024,768]{1,0:T(8,128)(2,1)} async-done(((bf16[1024,768]{1,0:T(8,128)(2,1)}), bf16[1024,768]{1,0:T(8,128)(2,1)}) %all-reduce.17.cloned.1.call-update) | async-done | bytes 1572880 | tf_op jit(solution)/shard_map/psum | solution.py:181
  426.5 18.6 %multiply_convert_fusion = (bf16[1024,1536]{1,0:T(8,128)(2,1)S(1)}, f32[1024,1536]{1,0:T(8,128)}, f32[1024,1536]{1,0:T(8,128)}) fusion(f32[1536]{0:T(1024)S(1)} %dynamic-slice_reduce_fusion.4, bf16[2,768,1536]{2,1,0:T(8,128)(2,1)S(1)} %bitcast.417, f32[1024,768]{1,0:T(8,128)S(1)} %get-tuple-element.545, f32[768]{0:T(1024)S(1)} %copy-done.104, ...), kind=kOutput, calls=%fused_computation.142 | convolution fusion | flops 2523660288 | bytes 21258240 | tf_op jit(solution)/shard_map/td,df->tf/dot_general | solution.py:190
  446.8 5.4 fusion.149
  452.2 21.7 %all-reduce.19.cloned.1.call-done = bf16[1024,768]{1,0:T(8,128)(2,1)} async-done(((bf16[1024,768]{1,0:T(8,128)(2,1)}), bf16[1024,768]{1,0:T(8,128)(2,1)}) %all-reduce.19.cloned.1.call-update) | async-done | bytes 1572880 | tf_op jit(solution)/shard_map/psum | solution.py:194
  484.4 9.5 fusion.211
  495.6 3.7 fusion.150
  503.6 8.0 convolution_bitcast_fusion.2
  511.6 9.5 all-reduce.21.cloned.1.call-done
  521.1 4.9 multiply_reduce_fusion.3
  541.2 36.4 %while.56 = (s32[]{:T(128)}, bf16[2,512,6,64]{1,3,2,0:T(8,128)(2,1)}, bf16[2,512,6,64]{1,3,2,0:T(8,128)(2,1)}, f32[2,512,6,64]{1,3,2,0:T(8,128)}, f32[2,6,512,51...) while((s32[]{:T(128)}, ...), condition=%wide.region_27.28_spmd, body=%wide.region_25.27_spmd.sunk | while | flops 1227224064 | bytes 94064864 | solution.py:276
  548.1 4.2 bitcast_dynamic-update-slice_fusion.8
  566.1 4.3 bitcast_dynamic-update-slice_fusion.8
  592.2 5.6 bitcast_convert_fusion.1
  598.0 7.9 convolution_bitcast_fusion
  608.8 4.3 convolution_bitcast_fusion.4
  613.1 6.5 all-reduce.23.cloned.1.call-done
  619.7 5.1 multiply_reduce_fusion.4
  627.1 9.6 fusion.212
  638.3 3.7 fusion.152
  642.1 5.6 convolution_bitcast_fusion.1
  647.8 7.4 pad_maximum_fusion.1
  655.3 4.9 convolution_bitcast_fusion.3
  663.8 4.8 multiply_reduce_fusion.5
  676.7 54.2 %while.57 = (s32[]{:T(128)}, bf16[2,512,6,64]{1,3,2,0:T(8,128)(2,1)}, bf16[2,512,6,64]{1,3,2,0:T(8,128)(2,1)}, f32[2,512,6,64]{1,3,2,0:T(8,128)}, bf16[2,512,6,6...) while((s32[]{:T(128)}, ...), condition=%wide.region_36.37_spmd, body=%wide.region_34.36_spmd.sunk | while | flops 1222512128 | bytes 87736576 | solution.py:276
  676.7 5.2 exponential_select_fusion.3
  681.9 7.6 fusion.310
  689.5 7.8 fusion.311
  703.8 5.2 exponential_select_fusion.3
  709.0 7.6 fusion.310
  716.6 7.8 fusion.311
  739.8 5.2 bitcast_convert_fusion
  745.3 8.5 pad_maximum_fusion
  772.1 736.8 %all-reduce.31.cloned.1.call-done = (f32[2,768,3,384]{3,1,2,0:T(8,128)}, f32[2,768,384]{2,1,0:T(8,128)}, f32[2,768,1536]{2,1,0:T(8,128)}, f32[2,768,1536]{2,1,0:T(8,128)}) async-done(((f32[2,768,3,384]{3,1,2,0:T(8,128)}, f32[2,768,384]{2,1,0:T(8,128)}, f32[2,768,1536]{2,1,0:T(8,128)}, f32[2,768,1536]{2,1,0:T(8,128)}), (f32[2,768,3,384]{3,1,2,0:T(8,128)}, f32[2,768,384]{2,1,0:T(8,128)}, ...) | async-done | bytes 28311568 | tf_op jit(solution)/shard_map/psum | solution.py:323
  1518.5 114.0 %all-reduce.29.cloned.1.call-done = f32[2,8448]{1,0:T(2,128)} async-done(((f32[2,8448]{1,0:T(2,128)}), f32[2,8448]{1,0:T(2,128)}) %all-reduce.29.cloned.1.call-update) | async-done | bytes 67600 | tf_op jit(solution)/shard_map/psum | solution.py:337
  1634.1 42.6 %psum.124 = f32[]{:T(128)} all-reduce(f32[]{:T(128)S(6)} %add.424), channel_id=1, replica_groups=mesh['dp'=16,'tensor'=2] {'dp','tensor'}, use_global_device_ids=true, to_apply=%region_46.47 | all-reduce | flops 1 | bytes 8 | tf_op jit(solution)/shard_map/psum | solution.py:337
  1687.8 39.3 %all-reduce = (f32[4,2]{1,0:T(4,128)S(1)}, f32[4,2]{1,0:T(4,128)S(1)}) all-reduce(f32[4,2]{1,0:T(4,128)S(1)} %pad_maximum_fusion.12, f32[4,2]{1,0:T(4,128)S(1)} %pad_maximum_fusion.11), channel_id=1, replica_groups=mesh['dp'=16,'tensor'=2] {'dp','tensor'}, use_global_device_ids=true, to_apply=%region_74.75 | all-reduce | flops 16 | bytes 128 | tf_op jit(solution)/shard_map/psum | solution.py:353
  (542 shorter events, 240.5 us)
Async XLA Ops:
  7.2 78.1 %all-gather.5.cloned.1.call-start = ((), (), s32[]{:S(2)}) async-start(), calls=%async_computation | async-start | bytes 3760128 | tf_op jit(solution)/shard_map/all_gather | solution.py:137
  9.0 134.3 %all-gather.7.cloned.1.call-start = ((), (), s32[]{:S(2)}) async-start(), calls=%async_computation.1 | async-start | bytes 1253376 | tf_op jit(solution)/shard_map/all_gather | solution.py:138
  10.6 155.7 %all-reduce.13.cloned.1.call-start = ((), (), s32[]{:S(2)}) async-start(), calls=%async_computation.2 | async-start | bytes 3145728 | tf_op jit(solution)/shard_map/psum | solution.py:181
  12.2 347.3 %copy-start.73 = (f32[768]{0:T(1024)}, f32[768]{0:T(1024)S(1)}, u32[]{:S(2)}) copy-start(f32[768]{0:T(1024)S(1)} %get-tuple-element.433) | copy-start | bytes 9220
  12.2 347.3 %copy-start.82 = (f32[768]{0:T(1024)}, f32[768]{0:T(1024)S(1)}, u32[]{:S(2)}) copy-start(f32[768]{0:T(1024)S(1)} %get-tuple-element.432) | copy-start | bytes 9220
  12.2 347.3 %copy-start.100 = (f32[768]{0:T(1024)}, f32[768]{0:T(1024)S(1)}, u32[]{:S(2)}) copy-start(f32[768]{0:T(1024)S(1)} %get-tuple-element.431) | copy-start | bytes 9220
  12.2 409.8 %copy-start.86 = (f32[768]{0:T(1024)}, f32[768]{0:T(1024)S(1)}, u32[]{:S(2)}) copy-start(f32[768]{0:T(1024)S(1)} %get-tuple-element.429) | copy-start | bytes 9220
  12.2 409.8 %copy-start.102 = (f32[768]{0:T(1024)}, f32[768]{0:T(1024)S(1)}, u32[]{:S(2)}) copy-start(f32[768]{0:T(1024)S(1)} %get-tuple-element.428) | copy-start | bytes 9220
  114.9 28.3 %copy-start.20 = (bf16[2,512,6,64]{1,3,2,0:T(8,128)(2,1)}, bf16[2,512,6,64]{1,3,2,0:T(8,128)(2,1)S(1)}, u32[]{:S(2)}) copy-start(bf16[2,512,6,64]{1,3,2,0:T(8,128)(2,1)S(1)} %get-tuple-element.1014) | copy-start | bytes 2359300
  114.9 31.9 %copy-start.69 = (f32[2,6,512]{2,1,0:T(8,128)}, f32[2,6,512]{2,1,0:T(8,128)S(1)}, u32[]{:S(2)}) copy-start(f32[2,6,512]{2,1,0:T(8,128)S(1)} %get-tuple-element.954) | copy-start | bytes 73732
  116.8 32.0 %copy-start.32 = (f32[2,48,1536]{2,1,0:T(8,128)S(1)}, f32[2,48,1536]{2,1,0:T(8,128)}, u32[]{:S(2)}) copy-start(f32[2,48,1536]{2,1,0:T(8,128)} %param.32) | copy-start | bytes 1769476
  143.3 23.1 %copy-start.10 = (bf16[1024,768]{1,0:T(8,128)(2,1)S(1)}, bf16[1024,768]{1,0:T(8,128)(2,1)}, u32[]{:S(2)}) copy-start(bf16[1024,768]{1,0:T(8,128)(2,1)} %param.26) | copy-start | bytes 4718596
  146.9 104.6 %all-gather.9.cloned.1.call-start = ((), (), s32[]{:S(2)}) async-start(), calls=%async_computation.3 | async-start | bytes 5013504 | tf_op jit(solution)/shard_map/all_gather | solution.py:139
  148.8 185.2 %all-gather.11.cloned.1.call-start = ((), (), s32[]{:S(2)}) async-start(), calls=%async_computation.4 | async-start | bytes 5013504 | tf_op jit(solution)/shard_map/all_gather | solution.py:140
  149.6 209.9 %all-reduce.15.cloned.1.call-start = ((), (), s32[]{:S(2)}) async-start(), calls=%async_computation.5 | async-start | bytes 3145728 | tf_op jit(solution)/shard_map/psum | solution.py:194
  150.5 100.9 %copy-start.116 = (f32[1536]{0:T(1024)}, f32[1536]{0:T(1024)S(1)}, u32[]{:S(2)}) copy-start(f32[1536]{0:T(1024)S(1)} %dynamic-slice_reduce_fusion.5) | copy-start | bytes 18436
  168.5 191.1 %copy-start.76 = (f32[1024]{0:T(1024)}, f32[1024]{0:T(1024)S(1)}, u32[]{:S(2)}) copy-start(f32[1024]{0:T(1024)S(1)} %broadcast_multiply_fusion.3) | copy-start | bytes 12292
  169.4 102.9 %copy-start.92 = (f32[1024]{0:T(1024)}, f32[1024]{0:T(1024)S(1)}, u32[]{:S(2)}) copy-start(f32[1024]{0:T(1024)S(1)} %multiply_reduce_fusion.13) | copy-start | bytes 12292
  169.4 190.2 %copy-start.84 = (f32[1024]{0:T(1024)}, f32[1024]{0:T(1024)S(1)}, u32[]{:S(2)}) copy-start(f32[1024]{0:T(1024)S(1)} %fusion.167) | copy-start | bytes 12292
  340.4 81.7 %all-reduce.17.cloned.1.call-start = ((), (), s32[]{:S(2)}) async-start(), calls=%async_computation.6 | async-start | bytes 3145728 | tf_op jit(solution)/shard_map/psum | solution.py:181
  363.2 58.9 %copy-start.78 = (f32[1024]{0:T(1024)}, f32[1024]{0:T(1024)S(1)}, u32[]{:S(2)}) copy-start(f32[1024]{0:T(1024)S(1)} %broadcast_multiply_fusion.2) | copy-start | bytes 12292
  363.7 58.4 %copy-start.89 = (f32[1024]{0:T(1024)}, f32[1024]{0:T(1024)S(1)}, u32[]{:S(2)}) copy-start(f32[1024]{0:T(1024)S(1)} %fusion.168) | copy-start | bytes 12292
  397.1 25.0 %copy-start.106 = (f32[768]{0:T(1024)S(1)}, f32[768]{0:T(1024)}, u32[]{:S(2)}) copy-start(f32[768]{0:T(1024)} %get-tuple-element.427) | copy-start | bytes 9220
  400.3 73.6 %all-reduce.19.cloned.1.call-start = ((), (), s32[]{:S(2)}) async-start(), calls=%async_computation.7 | async-start | bytes 3145728 | tf_op jit(solution)/shard_map/psum | solution.py:194
  425.8 19.4 %copy-start.3 = (f32[1024,768]{1,0:T(8,128)}, f32[1024,768]{1,0:T(8,128)S(1)}, u32[]{:S(2)}) copy-start(f32[1024,768]{1,0:T(8,128)S(1)} %get-tuple-element.545) | copy-start | bytes 9437188
  446.8 27.2 %copy-start.105 = (f32[768]{0:T(1024)S(1)}, f32[768]{0:T(1024)}, u32[]{:S(2)}) copy-start(f32[768]{0:T(1024)} %get-tuple-element.424) | copy-start | bytes 9220
  452.2 68.9 %all-reduce.21.cloned.1.call-start = ((), (), s32[]{:S(2)}) async-start(), calls=%async_computation.8 | async-start | bytes 3145728 | tf_op jit(solution)/shard_map/psum | solution.py:246
  481.4 14.2 slice-start.4
  484.4 11.2 slice-start.5
  499.3 120.3 %all-reduce.23.cloned.1.call-start = ((), (), s32[]{:S(2)}) async-start(), calls=%async_computation.9 | async-start | bytes 3145728 | tf_op jit(solution)/shard_map/psum | solution.py:293
  597.9 65.9 %all-reduce.25.cloned.1.call-start = ((), (), s32[]{:S(2)}) async-start(), calls=%async_computation.10 | async-start | bytes 3145728 | tf_op jit(solution)/shard_map/psum | solution.py:246
  613.1 11.7 copy-start.95
  625.2 13.1 slice-start.6
  627.1 11.3 slice-start.7
  642.1 125.4 %all-reduce.27.cloned.1.call-start = ((), (), s32[]{:S(2)}) async-start(), calls=%async_computation.11 | async-start | bytes 3145728 | tf_op jit(solution)/shard_map/psum | solution.py:293
  681.9 19.8 %slice-start = ((s8[6291456]{0:T(1024)(128)(4,1)}), s8[2097152]{0:T(1024)(128)(4,1)S(1)}, s32[]{:S(2)}) async-start(s8[6291456]{0:T(1024)(128)(4,1)} %bitcast.400), calls=%async_computation.14 | async-start | bytes 4194304 | tf_op jit(solution)/shard_map/while
  689.5 12.2 slice-start.1
  709.0 19.8 %slice-start = ((s8[6291456]{0:T(1024)(128)(4,1)}), s8[2097152]{0:T(1024)(128)(4,1)S(1)}, s32[]{:S(2)}) async-start(s8[6291456]{0:T(1024)(128)(4,1)} %bitcast.400), calls=%async_computation.14 | async-start | bytes 4194304 | tf_op jit(solution)/shard_map/while
  716.6 12.2 slice-start.1
  745.0 763.9 %all-reduce.31.cloned.1.call-start = ((), (), s32[]{:S(2)}) async-start(), calls=%async_computation.13 | async-start | bytes 56623104 | tf_op jit(solution)/shard_map/psum | solution.py:323
  763.9 868.6 %all-reduce.29.cloned.1.call-start = ((), (), s32[]{:S(2)}) async-start(), calls=%async_computation.12 | async-start | bytes 135168 | tf_op jit(solution)/shard_map/psum | solution.py:337
  767.5 910.6 %copy-start.47 = (f32[2,48,384]{2,1,0:T(8,128)S(1)}, f32[2,48,384]{2,1,0:T(8,128)}, u32[]{:S(2)}) copy-start(f32[2,48,384]{2,1,0:T(8,128)} %param.30) | copy-start | bytes 442372
  771.2 908.8 %copy-start.34 = (f32[2,48,1536]{2,1,0:T(8,128)S(1)}, f32[2,48,1536]{2,1,0:T(8,128)}, u32[]{:S(2)}) copy-start(f32[2,48,1536]{2,1,0:T(8,128)} %param.31) | copy-start | bytes 1769476
  771.2 908.8 %copy-start.66 = (f32[2,48,1536]{2,1,0:T(8,128)S(1)}, f32[2,48,1536]{2,1,0:T(8,128)}, u32[]{:S(2)}) copy-start(f32[2,48,1536]{2,1,0:T(8,128)} %param.38) | copy-start | bytes 1769476
  1508.9 173.1 %copy-start.33 = (f32[2,48,1536]{2,1,0:T(8,128)S(1)}, f32[2,48,1536]{2,1,0:T(8,128)}, u32[]{:S(2)}) copy-start(f32[2,48,1536]{2,1,0:T(8,128)} %param.32) | copy-start | bytes 1769476
  1682.0 47.4 %copy-start.42 = (f32[2,48,1536]{2,1,0:T(8,128)}, f32[2,48,1536]{2,1,0:T(8,128)S(1)}, u32[]{:S(2)}) copy-start(f32[2,48,1536]{2,1,0:T(8,128)S(1)} %get-tuple-element.528) | copy-start | bytes 1769476
  1682.0 47.4 %copy-start.43 = (f32[2,48,1536]{2,1,0:T(8,128)}, f32[2,48,1536]{2,1,0:T(8,128)S(1)}, u32[]{:S(2)}) copy-start(f32[2,48,1536]{2,1,0:T(8,128)S(1)} %get-tuple-element.529) | copy-start | bytes 1769476
  1685.2 45.4 %copy-start.44 = (f32[2,48,1536]{2,1,0:T(8,128)}, f32[2,48,1536]{2,1,0:T(8,128)S(1)}, u32[]{:S(2)}) copy-start(f32[2,48,1536]{2,1,0:T(8,128)S(1)} %get-tuple-element.530) | copy-start | bytes 1769476
  (111 other events, 434.2 us)
Sparse Core Ops, SparseCore 0:
  11.3 73.9 all-gather.4
  88.5 54.6 all-gather.6
  147.0 19.2 all-reduce.12
  169.8 81.6 all-gather.8
  255.0 78.9 all-gather.10
  340.5 19.0 all-reduce.14
  400.5 21.5 all-reduce.16
  452.3 21.5 all-reduce.18
  499.5 21.5 all-reduce.20
  598.0 21.5 all-reduce.22
  642.2 21.5 all-reduce.24
  745.1 21.5 all-reduce.26
  773.2 735.7 all-reduce.30
  1515.9 116.6 all-reduce.28
where the time goes:
time: 1750 us; the launch traced here: 1740 us
  waiting for transfers between devices  1190 us (68%)
  matrix products  238 us (14%)
  other arithmetic  120 us (7%)
  local copies, waits for them, and re-layouts  86.9 us (5%)
  blocking collectives  81.9 us (5%)
  between operations  20.9 us (1%)
    psum x1, waiting for transfers between devices, local(): lax.psum((big_totals[0], big_totals[1], big_totals[2], big_totals[3]), 'dp')  737 us
    psum x1, waiting for transfers between devices, local(): lax.psum((square_part, weight_square, small_partial), ('dp', 'tensor'))  114 us
    all_gather x1, waiting for transfers between devices, local(): lax.all_gather(up_weight.astype(jnp.bfloat16), 'dp', axis=1, tiled=True)  82.1 us
    all_gather x1, waiting for transfers between devices, local(): lax.all_gather(proj_weight.astype(jnp.bfloat16), 'dp', axis=1, tiled=True)  72.2 us
    all_gather x1, waiting for transfers between devices, local(): lax.all_gather(down_weight.astype(jnp.bfloat16), 'dp', axis=1, tiled=True)  61.6 us
    psum x1, blocking collectives, local(): lax.psum((square_part, weight_square, small_partial), ('dp', 'tensor'))  42.6 us
    psum x2, waiting for transfers between devices, local(): lax.psum(jnp.einsum('tf,df->td', act_low, down_full[layer_at], preferred_...  40.7 us
    dot_general x2, matrix products, local(): jnp.einsum('td,df->tf', first_low, up_full[layer_at], preferred_element_t...  39.4 us
  transfers between devices with their start and end apart: 14, of which 13 were waited for; matrix products, arithmetic and copies ran while one was open for 8% of the time, Pallas kernels for 0%

commit v1 on v0

--- a/solution.py
+++ b/solution.py
@@ -18,6 +18,28 @@
 step_count = 10.0
 norm_eps = 1e-06
 masked_score = -1e30
+
+
+def joined_along(blocks, dim):
+    blocks = jnp.moveaxis(blocks, 0, dim)
+    shape = blocks.shape
+    return blocks.reshape(*shape[:dim], shape[dim] * shape[dim + 1], *shape[dim + 2 :])
+
+
+def collect(shard, axis, dim):
+    size = lax.axis_size(axis)
+    pairs = [(i, (i + 1) % size) for i in range(size)]
+    back = [(b, a) for a, b in pairs]
+    lower, upper = ([], [])
+    for step in range(size - 1):
+        if step % 2 == 0:
+            lower.append(lax.ppermute(lower[-1] if lower else shard, axis, pairs))
+        else:
+            upper.append(lax.ppermute(upper[-1] if upper else shard, axis, back))
+    tiles = jnp.stack([*lower[::-1], shard, *upper])
+    shift = lax.axis_index(axis) - len(lower)
+    tiles = tiles[(jnp.arange(size) - shift) % size]
+    return joined_along(tiles, dim)
 
 
 def layer_norm(values, norm_gain, norm_shift):
@@ -134,7 +156,7 @@
     share_scale = 1.0 / lax.axis_size("tensor")
     tensor_rank = lax.axis_index("tensor")
     proj_full, out_full, up_full, down_full = (
-        lax.all_gather(proj_weight.astype(jnp.bfloat16), "dp", axis=1, tiled=True),
+        collect(proj_weight.astype(jnp.bfloat16), "dp", 1),
         lax.all_gather(out_weight.astype(jnp.bfloat16), "dp", axis=1, tiled=True),
         lax.all_gather(up_weight.astype(jnp.bfloat16), "dp", axis=1, tiled=True),
         lax.all_gather(down_weight.astype(jnp.bfloat16), "dp", axis=1, tiled=True),

time: 1750 us -> 1770 us (1.011)
  waiting for transfers between devices: 1190 us -> 1120 us
  starting transfers between devices: 0.8 us -> 59.4 us
  local copies, waits for them, and re-layouts: 86.9 us -> 116 us
    all_gather x1 -> x0, waiting for transfers between devices: 72.2 us -> none  [local(): lax.all_gather(proj_weight.astype(jnp.bfloat16), 'dp', axis=1, tiled=True)]
    ppermute x0 -> x15, starting transfers between devices: none -> 58.6 us  [the longest x7 45.6 us: collect(): upper.append(lax.ppermute(upper[-1] if upper else shard, axis, back))]
    ppermute x0 -> x15, waiting for transfers between devices: none -> 27.2 us  [the longest x8 20.2 us: collect(): lower.append(lax.ppermute(lower[-1] if lower else shard, axis, pairs))]
    all_gather x1, waiting for transfers between devices: 26.5 us -> 0.01 us  [local(): lax.all_gather(out_weight.astype(jnp.bfloat16), 'dp', axis=1, tiled=True)]
  transfers between devices with their start and end apart: 14 -> 28, of which waited for: 13 -> 20; matrix products, arithmetic and copies ran while one was open for 8% -> 9% of each run, Pallas kernels for 0% -> 0%
where the time goes in v1:
time: 1770 us; the launch traced here: 1760 us
  waiting for transfers between devices  1120 us (63%)
  matrix products  237 us (13%)
  other arithmetic  123 us (7%)
  local copies, waits for them, and re-layouts  116 us (7%)
  blocking collectives  81.9 us (5%)
  starting transfers between devices  59.4 us (3%)
  between operations  21 us (1%)
    psum x1, waiting for transfers between devices, local(): lax.psum((big_totals[0], big_totals[1], big_totals[2], big_totals[3]), 'dp')  737 us
    psum x1, waiting for transfers between devices, local(): lax.psum((square_part, weight_square, small_partial), ('dp', 'tensor'))  114 us
    all_gather x1, waiting for transfers between devices, local(): lax.all_gather(up_weight.astype(jnp.bfloat16), 'dp', axis=1, tiled=True)  82.3 us
    all_gather x1, waiting for transfers between devices, local(): lax.all_gather(down_weight.astype(jnp.bfloat16), 'dp', axis=1, tiled=True)  61.7 us
    ppermute x7, starting transfers between devices, collect(): upper.append(lax.ppermute(upper[-1] if upper else shard, axis, back))  45.6 us
    psum x1, blocking collectives, local(): lax.psum((square_part, weight_square, small_partial), ('dp', 'tensor'))  42.6 us
    dot_general x2, matrix products, local(): jnp.einsum('td,df->tf', first_low, up_full[layer_at], preferred_element_t...  39.5 us
    psum x1, blocking collectives, local(): update_square = lax.psum(update_square, ('dp', 'tensor'))  39.3 us
  transfers between devices with their start and end apart: 28, of which 20 were waited for; matrix products, arithmetic and copies ran while one was open for 9% of the time, Pallas kernels for 0%

profile of v1, /device:TPU:0, one launch (start us, length us, event | category | flops | bytes accessed | tf_op | source)
XLA Modules:
  0.0 1757.4 jit_solution(4504972746224771627)
XLA Ops:
  11.3 9.4 collective-permute-done
  20.7 5.6 collective-permute-start.8
  26.4 4.7 collective-permute-done.1
  44.7 6.4 collective-permute-start.10
  55.1 7.2 collective-permute-start.11
  66.8 8.9 collective-permute-start.12
  80.5 7.2 collective-permute-start.13
  93.9 6.1 collective-permute-start.14
  138.8 12.9 while.54
  161.9 17.0 all-reduce.13.cloned.1.call-done
  181.9 82.3 %all-gather.6.cloned.1.call-done = bf16[2,768,1536]{2,1,0:T(8,128)(2,1)} async-done(((bf16[2,48,1536]{2,1,0:T(8,128)(2,1)}), bf16[2,768,1536]{2,1,0:T(8,128)(2,1)}) %all-gather.6.cloned.1.call-update) | async-done | bytes 4718608 | tf_op jit(solution)/shard_map/all_gather | solution.py:161
  264.2 20.9 %multiply_convert_fusion.1 = (bf16[1024,1536]{1,0:T(8,128)(2,1)}, f32[1024,1536]{1,0:T(8,128)}, f32[1024,1536]{1,0:T(8,128)}) fusion(f32[1536]{0:T(1024)S(1)} %dynamic-slice_reduce_fusion.5, bf16[2,768,1536]{2,1,0:T(8,128)(2,1)} %all-gather.6.cloned.1.call-done, f32[768]{0:T(1024)S(1)} %copy-done.101, f32[768]{0:T(1024)S(1)} %get-tuple-element.490, ...), kind=kOutput, calls=%fused_computation.156 | convolution fusion | flops 2526806016 | bytes 21257216 | tf_op jit(solution)/shard_map/td,df->tf/dot_general | solution.py:212
  285.1 61.7 %all-gather.8.cloned.1.call-done = bf16[2,768,1536]{2,1,0:T(8,128)(2,1)} async-done(((bf16[2,48,1536]{2,1,0:T(8,128)(2,1)}), bf16[2,768,1536]{2,1,0:T(8,128)(2,1)}) %all-gather.8.cloned.1.call-update) | async-done | bytes 4718608 | tf_op jit(solution)/shard_map/all_gather | solution.py:162
  346.8 6.4 fusion.151
  356.2 16.2 all-reduce.15.cloned.1.call-done
  395.8 14.0 while.55
  415.1 21.7 %all-reduce.17.cloned.1.call-done = bf16[1024,768]{1,0:T(8,128)(2,1)} async-done(((bf16[1024,768]{1,0:T(8,128)(2,1)}), bf16[1024,768]{1,0:T(8,128)(2,1)}) %all-reduce.17.cloned.1.call-update) | async-done | bytes 1572880 | tf_op jit(solution)/shard_map/psum | solution.py:203
  441.2 18.7 %multiply_convert_fusion = (bf16[1024,1536]{1,0:T(8,128)(2,1)S(1)}, f32[1024,1536]{1,0:T(8,128)}, f32[1024,1536]{1,0:T(8,128)}) fusion(f32[1536]{0:T(1024)S(1)} %dynamic-slice_reduce_fusion.4, bf16[2,768,1536]{2,1,0:T(8,128)(2,1)S(1)} %bitcast.453, f32[1024,768]{1,0:T(8,128)S(1)} %get-tuple-element.603, f32[768]{0:T(1024)S(1)} %copy-done.105, ...), kind=kOutput, calls=%fused_computation.143 | convolution fusion | flops 2523660288 | bytes 21258240 | tf_op jit(solution)/shard_map/td,df->tf/dot_general | solution.py:212
  461.7 5.4 fusion.149
  467.2 21.7 %all-reduce.19.cloned.1.call-done = bf16[1024,768]{1,0:T(8,128)(2,1)} async-done(((bf16[1024,768]{1,0:T(8,128)(2,1)}), bf16[1024,768]{1,0:T(8,128)(2,1)}) %all-reduce.19.cloned.1.call-update) | async-done | bytes 1572880 | tf_op jit(solution)/shard_map/psum | solution.py:216
  499.5 9.5 fusion.214
  518.7 8.0 convolution_bitcast_fusion.2
  526.7 9.5 all-reduce.21.cloned.1.call-done
  536.2 4.9 multiply_reduce_fusion.3
  556.2 36.1 %while.56 = (s32[]{:T(128)}, bf16[2,512,6,64]{1,3,2,0:T(8,128)(2,1)}, bf16[2,512,6,64]{1,3,2,0:T(8,128)(2,1)}, f32[2,512,6,64]{1,3,2,0:T(8,128)}, f32[2,6,512,51...) while((s32[]{:T(128)}, ...), condition=%wide.region_27.28_spmd, body=%wide.region_25.27_spmd.sunk | while | flops 1227224064 | bytes 94064864 | solution.py:298
  607.0 5.6 bitcast_convert_fusion.1
  612.7 7.9 convolution_bitcast_fusion
  623.6 4.5 convolution_bitcast_fusion.5
  628.0 6.4 all-reduce.23.cloned.1.call-done
  634.4 5.4 multiply_reduce_fusion.4
  641.8 9.6 fusion.215
  656.9 5.6 convolution_bitcast_fusion.1
  662.6 7.4 pad_maximum_fusion.1
  670.1 4.8 convolution_bitcast_fusion.3
  678.6 4.8 multiply_reduce_fusion.5
  691.4 54.4 %while.57 = (s32[]{:T(128)}, bf16[2,512,6,64]{1,3,2,0:T(8,128)(2,1)}, bf16[2,512,6,64]{1,3,2,0:T(8,128)(2,1)}, f32[2,512,6,64]{1,3,2,0:T(8,128)}, bf16[2,512,6,6...) while((s32[]{:T(128)}, ...), condition=%wide.region_36.37_spmd, body=%wide.region_34.36_spmd.sunk | while | flops 1222512128 | bytes 87736576 | solution.py:298
  691.4 5.2 exponential_select_fusion.3
  696.6 7.6 fusion.317
  704.2 7.8 fusion.318
  718.5 5.2 exponential_select_fusion.3
  723.7 7.6 fusion.317
  731.3 7.8 fusion.318
  755.9 5.0 bitcast_convert_fusion
  761.3 8.5 pad_maximum_fusion
  788.2 736.6 %all-reduce.31.cloned.1.call-done = (f32[2,768,3,384]{3,1,2,0:T(8,128)}, f32[2,768,384]{2,1,0:T(8,128)}, f32[2,768,1536]{2,1,0:T(8,128)}, f32[2,768,1536]{2,1,0:T(8,128)}) async-done(((f32[2,768,3,384]{3,1,2,0:T(8,128)}, f32[2,768,384]{2,1,0:T(8,128)}, f32[2,768,1536]{2,1,0:T(8,128)}, f32[2,768,1536]{2,1,0:T(8,128)}), (f32[2,768,3,384]{3,1,2,0:T(8,128)}, f32[2,768,384]{2,1,0:T(8,128)}, ...) | async-done | bytes 28311568 | tf_op jit(solution)/shard_map/psum | solution.py:345
  1534.4 114.2 %all-reduce.29.cloned.1.call-done = f32[2,8448]{1,0:T(2,128)} async-done(((f32[2,8448]{1,0:T(2,128)}), f32[2,8448]{1,0:T(2,128)}) %all-reduce.29.cloned.1.call-update) | async-done | bytes 67600 | tf_op jit(solution)/shard_map/psum | solution.py:359
  1650.1 42.6 %psum.124 = f32[]{:T(128)} all-reduce(f32[]{:T(128)S(6)} %add.450), channel_id=1, replica_groups=mesh['dp'=16,'tensor'=2] {'dp','tensor'}, use_global_device_ids=true, to_apply=%region_46.47 | all-reduce | flops 1 | bytes 8 | tf_op jit(solution)/shard_map/psum | solution.py:359
  1703.8 39.3 %all-reduce = (f32[4,2]{1,0:T(4,128)S(1)}, f32[4,2]{1,0:T(4,128)S(1)}) all-reduce(f32[4,2]{1,0:T(4,128)S(1)} %pad_maximum_fusion.12, f32[4,2]{1,0:T(4,128)S(1)} %pad_maximum_fusion.11), channel_id=1, replica_groups=mesh['dp'=16,'tensor'=2] {'dp','tensor'}, use_global_device_ids=true, to_apply=%region_74.75 | all-reduce | flops 16 | bytes 128 | tf_op jit(solution)/shard_map/psum | solution.py:375
  (595 shorter events, 326.8 us)
Async XLA Ops:
  7.2 98.5 %copy-start.28 = (f32[2,48,3,384]{3,1,2,0:T(8,128)S(1)}, f32[2,48,3,384]{3,1,2,0:T(8,128)}, u32[]{:S(2)}) copy-start(f32[2,48,3,384]{3,1,2,0:T(8,128)} %param.29) | copy-start | bytes 1327108
  7.2 147.5 %all-gather.4.cloned.1.call-start = ((), (), s32[]{:S(2)}) async-start(), calls=%async_computation | async-start | bytes 1253376 | tf_op jit(solution)/shard_map/all_gather | solution.py:160
  8.3 12.4 collective-permute-start
  20.7 10.3 collective-permute-start.1
  20.7 14.1 collective-permute-start.8
  31.1 11.1 collective-permute-start.2
  34.8 9.9 collective-permute-start.9
  42.2 9.6 collective-permute-start.3
  44.7 10.4 collective-permute-start.10
  51.8 10.5 collective-permute-start.4
  54.6 124.3 %all-reduce.13.cloned.1.call-start = ((), (), s32[]{:S(2)}) async-start(), calls=%async_computation.1 | async-start | bytes 3145728 | tf_op jit(solution)/shard_map/psum | solution.py:203
  55.1 11.6 collective-permute-start.11
  62.3 13.4 collective-permute-start.5
  64.1 308.4 %copy-start.74 = (f32[768]{0:T(1024)}, f32[768]{0:T(1024)S(1)}, u32[]{:S(2)}) copy-start(f32[768]{0:T(1024)S(1)} %get-tuple-element.491) | copy-start | bytes 9220
  64.1 308.4 %copy-start.83 = (f32[768]{0:T(1024)}, f32[768]{0:T(1024)S(1)}, u32[]{:S(2)}) copy-start(f32[768]{0:T(1024)S(1)} %get-tuple-element.490) | copy-start | bytes 9220
  64.1 372.7 %copy-start.87 = (f32[768]{0:T(1024)}, f32[768]{0:T(1024)S(1)}, u32[]{:S(2)}) copy-start(f32[768]{0:T(1024)S(1)} %get-tuple-element.487) | copy-start | bytes 9220
  66.8 13.7 collective-permute-start.12
  75.7 14.0 collective-permute-start.6
  80.5 13.4 collective-permute-start.13
  89.7 10.3 collective-permute-start.7
  93.9 16.8 collective-permute-start.14
  158.2 106.0 %all-gather.6.cloned.1.call-start = ((), (), s32[]{:S(2)}) async-start(), calls=%async_computation.2 | async-start | bytes 5013504 | tf_op jit(solution)/shard_map/all_gather | solution.py:161
  160.1 186.7 %all-gather.8.cloned.1.call-start = ((), (), s32[]{:S(2)}) async-start(), calls=%async_computation.3 | async-start | bytes 5013504 | tf_op jit(solution)/shard_map/all_gather | solution.py:162
  160.9 211.5 %all-reduce.15.cloned.1.call-start = ((), (), s32[]{:S(2)}) async-start(), calls=%async_computation.4 | async-start | bytes 3145728 | tf_op jit(solution)/shard_map/psum | solution.py:216
  161.9 102.3 %copy-start.119 = (f32[1536]{0:T(1024)}, f32[1536]{0:T(1024)S(1)}, u32[]{:S(2)}) copy-start(f32[1536]{0:T(1024)S(1)} %dynamic-slice_reduce_fusion.5) | copy-start | bytes 18436
  178.9 85.3 %copy-start.101 = (f32[768]{0:T(1024)S(1)}, f32[768]{0:T(1024)}, u32[]{:S(2)}) copy-start(f32[768]{0:T(1024)} %get-tuple-element.489) | copy-start | bytes 9220
  181.0 191.4 %copy-start.77 = (f32[1024]{0:T(1024)}, f32[1024]{0:T(1024)S(1)}, u32[]{:S(2)}) copy-start(f32[1024]{0:T(1024)S(1)} %broadcast_multiply_fusion.3) | copy-start | bytes 12292
  181.9 103.2 %copy-start.93 = (f32[1024]{0:T(1024)}, f32[1024]{0:T(1024)S(1)}, u32[]{:S(2)}) copy-start(f32[1024]{0:T(1024)S(1)} %multiply_reduce_fusion.13) | copy-start | bytes 12292
  181.9 190.5 %copy-start.85 = (f32[1024]{0:T(1024)}, f32[1024]{0:T(1024)S(1)}, u32[]{:S(2)}) copy-start(f32[1024]{0:T(1024)S(1)} %fusion.166) | copy-start | bytes 12292
  353.2 83.6 %all-reduce.17.cloned.1.call-start = ((), (), s32[]{:S(2)}) async-start(), calls=%async_computation.5 | async-start | bytes 3145728 | tf_op jit(solution)/shard_map/psum | solution.py:203
  376.1 60.7 %copy-start.79 = (f32[1024]{0:T(1024)}, f32[1024]{0:T(1024)S(1)}, u32[]{:S(2)}) copy-start(f32[1024]{0:T(1024)S(1)} %broadcast_multiply_fusion.2) | copy-start | bytes 12292
  376.7 60.1 %copy-start.90 = (f32[1024]{0:T(1024)}, f32[1024]{0:T(1024)S(1)}, u32[]{:S(2)}) copy-start(f32[1024]{0:T(1024)S(1)} %fusion.167) | copy-start | bytes 12292
  411.8 25.0 %copy-start.107 = (f32[768]{0:T(1024)S(1)}, f32[768]{0:T(1024)}, u32[]{:S(2)}) copy-start(f32[768]{0:T(1024)} %get-tuple-element.485) | copy-start | bytes 9220
  415.1 73.8 %all-reduce.19.cloned.1.call-start = ((), (), s32[]{:S(2)}) async-start(), calls=%async_computation.6 | async-start | bytes 3145728 | tf_op jit(solution)/shard_map/psum | solution.py:216
  461.7 27.2 %copy-start.106 = (f32[768]{0:T(1024)S(1)}, f32[768]{0:T(1024)}, u32[]{:S(2)}) copy-start(f32[768]{0:T(1024)} %get-tuple-element.482) | copy-start | bytes 9220
  467.1 69.1 %all-reduce.21.cloned.1.call-start = ((), (), s32[]{:S(2)}) async-start(), calls=%async_computation.7 | async-start | bytes 3145728 | tf_op jit(solution)/shard_map/psum | solution.py:268
  514.5 119.9 %all-reduce.23.cloned.1.call-start = ((), (), s32[]{:S(2)}) async-start(), calls=%async_computation.8 | async-start | bytes 3145728 | tf_op jit(solution)/shard_map/psum | solution.py:315
  612.7 65.9 %all-reduce.25.cloned.1.call-start = ((), (), s32[]{:S(2)}) async-start(), calls=%async_computation.9 | async-start | bytes 3145728 | tf_op jit(solution)/shard_map/psum | solution.py:268
  656.8 126.8 %all-reduce.27.cloned.1.call-start = ((), (), s32[]{:S(2)}) async-start(), calls=%async_computation.10 | async-start | bytes 3145728 | tf_op jit(solution)/shard_map/psum | solution.py:315
  761.0 763.8 %all-reduce.31.cloned.1.call-start = ((), (), s32[]{:S(2)}) async-start(), calls=%async_computation.12 | async-start | bytes 56623104 | tf_op jit(solution)/shard_map/psum | solution.py:345
  780.0 868.6 %all-reduce.29.cloned.1.call-start = ((), (), s32[]{:S(2)}) async-start(), calls=%async_computation.11 | async-start | bytes 135168 | tf_op jit(solution)/shard_map/psum | solution.py:359
  783.6 910.5 %copy-start.51 = (f32[2,48,384]{2,1,0:T(8,128)S(1)}, f32[2,48,384]{2,1,0:T(8,128)}, u32[]{:S(2)}) copy-start(f32[2,48,384]{2,1,0:T(8,128)} %param.30) | copy-start | bytes 442372
  787.3 908.7 %copy-start.36 = (f32[2,48,1536]{2,1,0:T(8,128)S(1)}, f32[2,48,1536]{2,1,0:T(8,128)}, u32[]{:S(2)}) copy-start(f32[2,48,1536]{2,1,0:T(8,128)} %param.31) | copy-start | bytes 1769476
  787.3 908.7 %copy-start.67 = (f32[2,48,1536]{2,1,0:T(8,128)S(1)}, f32[2,48,1536]{2,1,0:T(8,128)}, u32[]{:S(2)}) copy-start(f32[2,48,1536]{2,1,0:T(8,128)} %param.38) | copy-start | bytes 1769476
  1524.8 173.3 %copy-start.35 = (f32[2,48,1536]{2,1,0:T(8,128)S(1)}, f32[2,48,1536]{2,1,0:T(8,128)}, u32[]{:S(2)}) copy-start(f32[2,48,1536]{2,1,0:T(8,128)} %param.32) | copy-start | bytes 1769476
  1698.0 47.4 %copy-start.43 = (f32[2,48,1536]{2,1,0:T(8,128)}, f32[2,48,1536]{2,1,0:T(8,128)S(1)}, u32[]{:S(2)}) copy-start(f32[2,48,1536]{2,1,0:T(8,128)S(1)} %get-tuple-element.586) | copy-start | bytes 1769476
  1698.0 47.4 %copy-start.44 = (f32[2,48,1536]{2,1,0:T(8,128)}, f32[2,48,1536]{2,1,0:T(8,128)S(1)}, u32[]{:S(2)}) copy-start(f32[2,48,1536]{2,1,0:T(8,128)S(1)} %get-tuple-element.587) | copy-start | bytes 1769476
  1701.2 45.4 %copy-start.45 = (f32[2,48,1536]{2,1,0:T(8,128)}, f32[2,48,1536]{2,1,0:T(8,128)S(1)}, u32[]{:S(2)}) copy-start(f32[2,48,1536]{2,1,0:T(8,128)S(1)} %get-tuple-element.588) | copy-start | bytes 1769476
  (129 other events, 632.0 us)
Sparse Core Ops, SparseCore 0:
  54.8 59.7 all-gather.3
  158.3 20.5 all-reduce.12
  182.5 81.6 all-gather.5
  267.7 79.0 all-gather.7
  353.4 19.0 all-reduce.14
  415.2 21.5 all-reduce.16
  467.2 21.5 all-reduce.18
  514.6 21.5 all-reduce.20
  612.8 21.5 all-reduce.22
  657.0 21.5 all-reduce.24
  761.1 21.5 all-reduce.26
  789.0 735.7 all-reduce.30
  1531.8 116.6 all-reduce.28
